TPU v7x, 32 devices: a whole 2x2x4 slice. The times are simulated.
32 devices in a mesh: dp: 8 (over z, core), clus: 4 (over y, x).
Axes of the slice: x: 2, y: 2, z: 4, core: 2. Of those that a mesh axis runs over, the one named last changes fastest.
Arguments:
- rows: bfloat16 [8192, 1024], P(('dp', 'clus')), may hold values from -8 to 8
- fine_assign: int32 [8192], P(('dp', 'clus')), may hold values from 0 to 8191, as said below
- parent1: int32 [8192], P(('dp', 'clus')), may hold values from 0 to 2047, as said below
- parent2: int32 [2048], P('dp'), may hold values from 0 to 511
- parent3: int32 [512], replicated, may hold values from 0 to 63
- shrink: float32 [4], replicated, may hold values from 0.5 to 2
Outputs:
- fine_centroids: bfloat16 [8192, 1024], P(('dp', 'clus'))
- mid_centroids: bfloat16 [2048, 1024], P(('dp', 'clus'))
- coarse_centroids: bfloat16 [512, 1024], P(('dp', 'clus'))
- spread: float32 [8192], P(('dp', 'clus'))
Inputs may be any that keep to these rules, and one draw needn't show every extreme that they name: `fine_assign`: devices are numbered d = dp index * 4 + clus index, and fine centroid k is owned by device k // 256. Every row of device d names a fine centroid owned by a device of the same dp index. At most 128 rows of one device name centroids of one owner, and in every dp group some owner is named by exactly 128 rows of each device of the group. parent1[k] is one of the 256 second-level centroids g * 256 to g * 256 + 255, with g = k // 1024.
All inputs are finite; a program needn't handle non-finite values.
Results may differ from a plain program's by a relative error of at most 0.0035.
Values may be sent and summed in bfloat16 or wider, within the bound.
A program may use at most 64 MiB of HBM per device.

v0:
```python
import jax
import jax.numpy as jnp
from jax import lax
from jax.sharding import PartitionSpec as P

K4 = 64


HIGH = lax.Precision.HIGHEST


def shrunk(sums, counts, prior, weight):
    return (sums + weight * prior) / (counts + weight)[:, None]


def local(rows, fine_assign, parent1, parent2, parent3, shrink):
    groups = lax.axis_size("clus")
    dp_count = lax.axis_size("dp")
    devices = groups * dp_count
    clus_index = lax.axis_index("clus")
    dp_index = lax.axis_index("dp")
    count = rows.shape[0]
    width = rows.shape[1]
    fine_dev = parent1.shape[0]
    middle_dp = parent2.shape[0]
    third = parent3.shape[0]
    slots = 2 * count // groups
    total = count * devices
    weight_top = shrink[0] * (total / K4)
    weight_third = shrink[1] * (total / third)
    weight_middle = shrink[2] * (total / (middle_dp * dp_count))
    weight_fine = shrink[3] * (total / (fine_dev * devices))
    local_ids = fine_assign - dp_index * groups * fine_dev
    target = local_ids // fine_dev
    within = local_ids - target * fine_dev
    target_hot = (target[:, None] == jnp.arange(groups)[None, :]).astype(jnp.bfloat16)
    earlier = (jnp.arange(count)[:, None] > jnp.arange(count)[None, :]).astype(jnp.bfloat16)
    before = jnp.dot(earlier, target_hot, preferred_element_type=jnp.float32)
    rank = jnp.sum(before * target_hot.astype(jnp.float32), axis=1).astype(jnp.int32)
    slot_of = target * slots + rank
    source = (
        jnp.full((groups * slots,), count, jnp.int32)
        .at[slot_of]
        .set(jnp.arange(count, dtype=jnp.int32))
    )
    padded = jnp.concatenate([rows, jnp.zeros((1, width), jnp.bfloat16)], axis=0)
    send_rows = padded[source].reshape(groups, slots, width)
    send_ids = jnp.concatenate([within, jnp.full((1,), -1, jnp.int32)])[source].reshape(
        groups, slots
    )
    got_rows, got_ids = (
        lax.all_to_all(send_rows, "clus", split_axis=0, concat_axis=0, tiled=True),
        lax.all_to_all(send_ids, "clus", split_axis=0, concat_axis=0, tiled=True),
    )
    got_rows = got_rows.reshape(groups * slots, width)
    got_ids = got_ids.reshape(groups * slots)
    member = (got_ids[:, None] == jnp.arange(fine_dev)[None, :]).astype(jnp.bfloat16)
    contract = (((0,), (0,)), ((), ()))
    fine_sums = lax.dot_general(member, got_rows, contract, preferred_element_type=jnp.float32)
    fine_counts = jnp.sum(member.astype(jnp.float32), axis=0)
    middle_local = parent1 - dp_index * middle_dp
    child_hot = (jnp.arange(middle_dp)[:, None] == middle_local[None, :]).astype(jnp.float32)
    middle_part = jnp.dot(child_hot, fine_sums, precision=HIGH)
    middle_tally = jnp.dot(child_hot, fine_counts, precision=HIGH)
    share = middle_dp // groups
    offset = clus_index * share
    middle_sums, middle_counts = (
        lax.psum_scatter(middle_part, "clus", scatter_dimension=0, tiled=True),
        lax.psum_scatter(middle_tally, "clus", scatter_dimension=0, tiled=True),
    )
    own_parent2 = lax.dynamic_slice_in_dim(parent2, offset, share, 0)
    third_share = third // devices
    third_start = (dp_index * groups + clus_index) * third_share
    third_hot = (jnp.arange(third)[:, None] == own_parent2[None, :]).astype(jnp.float32)
    third_part = jnp.dot(third_hot, middle_sums, precision=HIGH)
    third_tally = jnp.dot(third_hot, middle_counts, precision=HIGH)
    third_sums, third_counts = lax.psum((third_part, third_tally), ("dp", "clus"))
    top_hot = (jnp.arange(K4)[:, None] == parent3[None, :]).astype(jnp.float32)
    top_sums = jnp.dot(top_hot, third_sums, precision=HIGH)
    top_counts = jnp.dot(top_hot, third_counts, precision=HIGH)
    center = jnp.sum(top_sums, axis=0) / total
    top_means = shrunk(top_sums, top_counts, center[None, :], weight_top)
    third_means = shrunk(
        third_sums, third_counts, jnp.dot(top_hot.T, top_means, precision=HIGH), weight_third
    )
    third_out = lax.dynamic_slice_in_dim(third_means, third_start, third_share, 0)
    parent_hot = (own_parent2[:, None] == jnp.arange(third)[None, :]).astype(jnp.float32)
    middle_out = shrunk(
        middle_sums, middle_counts, jnp.dot(parent_hot, third_means, precision=HIGH), weight_middle
    )
    middle_means = lax.all_gather(middle_out, "clus", axis=0, tiled=True)
    fine_means = shrunk(
        fine_sums, fine_counts, jnp.dot(child_hot.T, middle_means, precision=HIGH), weight_fine
    )
    fine_out = fine_means.astype(jnp.bfloat16)
    back = jnp.dot(member, fine_out, preferred_element_type=jnp.float32)
    diff = got_rows.astype(jnp.float32) - back
    row_error = jnp.sum(diff * diff, axis=1)
    spread = jnp.sum(member.astype(jnp.float32) * row_error[:, None], axis=0) / (
        width * (fine_counts + 1.0)
    )
    return (fine_out, middle_out.astype(jnp.bfloat16), third_out.astype(jnp.bfloat16), spread)


def solution(mesh):
    placed = (P(("dp", "clus"), None), P(("dp", "clus")), P(("dp", "clus")), P("dp"), P(), P())
    return jax.shard_map(
        local,
        mesh=mesh,
        in_specs=placed,
        out_specs=(
            P(("dp", "clus"), None),
            P(("dp", "clus"), None),
            P(("dp", "clus"), None),
            P(("dp", "clus")),
        ),
        check_vma=False,
    )
```

profile of v0, /device:TPU:0, one launch (start us, length us, event | category | flops | bytes accessed | tf_op | source)
XLA Modules:
  0.0 254.0 jit_solution(13841841108507027083)
XLA Ops:
  7.2 0.7 multiply_subtract_fusion
  7.9 0.2 fusion.5
  8.2 1.4 scatter_custom_fusion
  9.6 4.7 %gather_fusion = s32[512]{0:T(512)} fusion(s32[257]{0:T(512)S(1)} %pad_add_fusion, s32[1024]{0:T(1024)S(1)} %pad_clamp_fusion), kind=kCustom, calls=%fused_computation | custom fusion | bytes 6144 | tf_op jit(solution)/shard_map/gather | solution.py:48
  14.2 5.2 %all-to-all-start = ((s32[4,1,128]{2,1,0:T(1,128)}), s32[4,1,128]{2,1,0:T(1,128)S(1)}, u32[]{:S(2)}, u32[]{:S(2)}) async-start(s32[4,1,128]{2,1,0:T(1,128)} %bitcast), calls=%async_computation | async-start | bytes 4096 | tf_op jit(solution)/shard_map/all_to_all | solution.py:53
  19.5 2.8 %gather_fusion.1 = bf16[512,1024]{1,0:T(8,128)(2,1)} fusion(bf16[257,1024]{1,0:T(8,128)(2,1)S(1)} %concatenate.7, s32[1024]{0:T(1024)S(1)} %pad_clamp_fusion), kind=kCustom, calls=%fused_computation.1 | custom fusion | bytes 2099200 | tf_op jit(solution)/shard_map/gather | solution.py:47
  22.3 1.8 all-to-all-done
  24.0 3.5 %all-to-all-start.1 = ((bf16[4,128,1024]{2,1,0:T(8,128)(2,1)}), bf16[4,128,1024]{2,1,0:T(8,128)(2,1)S(1)}, u32[]{:S(2)}, u32[]{:S(2)}) async-start(bf16[4,128,1024]{2,1,0:T(8,128)(2,1)} %bitcast.2), calls=%async_computation.1 | async-start | bytes 2097152 | tf_op jit(solution)/shard_map/all_to_all | solution.py:52
  27.6 12.4 %all-to-all-done.1 = bf16[4,128,1024]{2,1,0:T(8,128)(2,1)S(1)} async-done(((bf16[4,128,1024]{2,1,0:T(8,128)(2,1)}), bf16[4,128,1024]{2,1,0:T(8,128)(2,1)S(1)}, u32[]{:S(2)}, u32[]{:S(2)}) %all-to-all-start.1) | async-done | bytes 1048608 | tf_op jit(solution)/shard_map/all_to_all | solution.py:52
  40.0 0.6 fusion.9
  40.7 1.7 fusion.15
  42.4 0.6 fusion.36
  45.0 0.6 dynamic-slice
  47.0 23.7 %reduce-scatter.2.cloned.1.call-done = f32[64,1024]{1,0:T(8,128)} async-done(((f32[256,1024]{1,0:T(8,128)}), f32[64,1024]{1,0:T(8,128)}) %reduce-scatter.2.cloned.1.call-update) | async-done | bytes 262160 | tf_op jit(solution)/shard_map/reduce_scatter | solution.py:68
  70.7 3.2 %fusion.13 = f32[512,1024]{1,0:T(8,128)} fusion(f32[64,1024]{1,0:T(8,128)} %reduce-scatter.2.cloned.1.call-done, s32[64]{0:T(128)S(1)} %dynamic_slice.6), kind=kOutput, calls=%fused_computation.26 | convolution fusion | flops 402685952 | bytes 2359552 | tf_op jit(solution)/shard_map/dot_general | solution.py:75
  74.0 0.1 convert_reduce_fusion
  74.2 0.2 fusion.14
  74.4 9.0 %all-reduce.1 = f32[256]{0:T(256)S(1)} all-reduce(f32[256]{0:T(256)S(1)} %bitcast.39), channel_id=3, replica_groups=mesh['dp'=8,'clus'=4] {'clus'}, use_global_device_ids=true, to_apply=%region_6.7.clone | all-reduce | flops 256 | bytes 2048
  83.4 0.2 fusion.12
  83.6 39.4 %psum.15 = f32[512]{0:T(512)S(1)} all-reduce(f32[512]{0:T(512)S(1)} %bitcast.38), channel_id=1, replica_groups=mesh['dp'=8,'clus'=4] {'dp','clus'}, use_global_device_ids=true, to_apply=%region_7.8 | all-reduce | flops 512 | bytes 4096 | tf_op jit(solution)/shard_map/psum | solution.py:77
  123.2 87.8 %all-reduce.4.cloned.1.call-done = f32[512,1024]{1,0:T(8,128)} async-done(((f32[512,1024]{1,0:T(8,128)}), f32[512,1024]{1,0:T(8,128)}) %all-reduce.4.cloned.1.call-update) | async-done | bytes 2097168 | tf_op jit(solution)/shard_map/psum | solution.py:77
  210.9 2.7 %fusion.37 = (f32[1024]{0:T(1024)S(1)}, f32[64,1024]{1,0:T(8,128)S(1)}) fusion(f32[512,1024]{1,0:T(8,128)} %all-reduce.4.cloned.1.call-done, s32[512]{0:T(512)S(1)} %copy-done.5), kind=kOutput, calls=%fused_computation.71 | convolution fusion | flops 402750464 | bytes 2365440 | tf_op jit(solution)/shard_map/dot_general | solution.py:79
  213.7 1.3 add_divide_fusion
  214.9 1.3 copy-done
  216.3 1.7 fusion.38
  218.0 0.7 broadcast_add_fusion.1
  218.7 1.5 dynamic-slice_convert_fusion
  220.1 23.3 %all-gather.2.cloned.1.call-done = f32[256,1024]{1,0:T(8,128)} async-done(((f32[64,1024]{1,0:T(8,128)}), f32[256,1024]{1,0:T(8,128)}) %all-gather.2.cloned.1.call-update) | async-done | bytes 1048592 | tf_op jit(solution)/shard_map/all_gather | solution.py:91
  243.4 2.6 %fusion.2 = bf16[256,1024]{1,0:T(8,128)(2,1)S(1)} fusion(f32[256,1024]{1,0:T(8,128)S(1)} %fusion.9, f32[256,1024]{1,0:T(8,128)} %all-gather.2.cloned.1.call-done, f32[256]{0:T(256)S(1)} %broadcast_add_fusion.1, f32[]{:T(128)} %bitcast.4, s32[256]{0:T(256)S(1)} %broadcast_subtract_fusion), kind=kOutput, calls=%fused_computation.8 | convolution fusion | flops 806420480 | bytes 2623492 | tf_op jit(solution)/shard_map/dot_general | solution.py:93
  246.1 0.6 multiply_reduce_fusion
  246.6 0.2 fusion.7
  246.9 0.6 multiply_divide_fusion
  (37 shorter events, 0.6 us)
Async XLA Ops:
  7.2 12.3 %copy-start.3 = (bf16[256,1024]{1,0:T(8,128)(2,1)S(1)}, bf16[256,1024]{1,0:T(8,128)(2,1)}, u32[]{:S(2)}) copy-start(bf16[256,1024]{1,0:T(8,128)(2,1)} %param.6) | copy-start | bytes 1572868
  14.2 9.8 %all-to-all-start = ((s32[4,1,128]{2,1,0:T(1,128)}), s32[4,1,128]{2,1,0:T(1,128)S(1)}, u32[]{:S(2)}, u32[]{:S(2)}) async-start(s32[4,1,128]{2,1,0:T(1,128)} %bitcast), calls=%async_computation | async-start | bytes 4096 | tf_op jit(solution)/shard_map/all_to_all | solution.py:53
  22.3 5.3 %copy-start.6 = (s32[256]{0:T(256)S(1)}, s32[256]{0:T(256)}, u32[]{:S(2)}) copy-start(s32[256]{0:T(256)} %param.8) | copy-start | bytes 3076
  24.0 16.0 %all-to-all-start.1 = ((bf16[4,128,1024]{2,1,0:T(8,128)(2,1)}), bf16[4,128,1024]{2,1,0:T(8,128)(2,1)S(1)}, u32[]{:S(2)}, u32[]{:S(2)}) async-start(bf16[4,128,1024]{2,1,0:T(8,128)(2,1)} %bitcast.2), calls=%async_computation.1 | async-start | bytes 2097152 | tf_op jit(solution)/shard_map/all_to_all | solution.py:52
  27.6 43.2 %reduce-scatter.2.cloned.1.call-start = ((), (), s32[]{:S(2)}) async-start(), calls=%async_computation.3 | async-start | bytes 1310720 | tf_op jit(solution)/shard_map/reduce_scatter | solution.py:68
  40.6 1.8 copy-start.4
  40.6 4.4 %copy-start.9 = (u32[32]{0:T(128)S(1)}, u32[32]{0:T(128)}, u32[]{:S(2)}) copy-start(u32[32]{0:T(128)} %constant.74) | copy-start | bytes 388
  40.6 5.6 %copy-start.7 = (s32[256]{0:T(256)S(1)}, s32[256]{0:T(256)}, u32[]{:S(2)}) copy-start(s32[256]{0:T(256)} %param.9) | copy-start | bytes 3076
  42.4 168.6 %all-reduce.4.cloned.1.call-start = ((), (), s32[]{:S(2)}) async-start(), calls=%async_computation.4 | async-start | bytes 4194304 | tf_op jit(solution)/shard_map/psum | solution.py:77
  47.0 76.1 %copy-start.5 = (s32[512]{0:T(512)S(1)}, s32[512]{0:T(512)}, u32[]{:S(2)}) copy-start(s32[512]{0:T(512)} %param.10) | copy-start | bytes 6148
  74.0 169.4 %all-gather.2.cloned.1.call-start = ((), (), s32[]{:S(2)}) async-start(), calls=%async_computation.5 | async-start | bytes 1310720 | tf_op jit(solution)/shard_map/all_gather | solution.py:91
  210.9 2.7 %copy-start.1 = (f32[512,1024]{1,0:T(8,128)S(1)}, f32[512,1024]{1,0:T(8,128)}, u32[]{:S(2)}) copy-start(f32[512,1024]{1,0:T(8,128)} %all-reduce.4.cloned.1.call-done) | copy-start | bytes 6291460
  213.7 2.6 %copy-start.2 = (f32[64,1024]{1,0:T(8,128)S(1)}, f32[64,1024]{1,0:T(8,128)}, u32[]{:S(2)}) copy-start(f32[64,1024]{1,0:T(8,128)} %reduce-scatter.2.cloned.1.call-done) | copy-start | bytes 786436
  214.9 1.4 copy-start
  246.1 1.4 copy-start.8
Sparse Core Ops, SparseCore 0:
  42.5 28.1 reduce-scatter.1
  76.1 134.8 all-reduce.3
  218.1 25.2 all-gather.1
where the time goes:
time: 254 us
  waiting for transfers between devices  149 us (59%)
  blocking collectives  48.4 us (19%)
  between operations  17.3 us (7%)
  matrix products  15.1 us (6%)
  local copies, waits for them, and re-layouts  13 us (5%)
  starting transfers between devices  8.83 us (3%)
    psum x1, waiting for transfers between devices, local(): lax.psum((third_part, third_tally), ('dp', 'clus'))  87.8 us
    psum x1, blocking collectives, local(): lax.psum((third_part, third_tally), ('dp', 'clus'))  39.4 us
    reduce_scatter x1, waiting for transfers between devices, local(): lax.psum_scatter(middle_part, 'clus', scatter_dimension=0, tiled=True)  23.7 us
    all_gather x1, waiting for transfers between devices, local(): middle_means = lax.all_gather(middle_out, 'clus', axis=0, tiled=True)  23.3 us
    all_to_all x1, waiting for transfers between devices, local(): lax.all_to_all(send_rows, 'clus', split_axis=0, concat_axis=0, tiled=True)  12.4 us
    unnamed x1, blocking collectives  8.99 us
    all_to_all x1, starting transfers between devices, local(): lax.all_to_all(send_ids, 'clus', split_axis=0, concat_axis=0, tiled=True)  5.19 us
  transfers between devices with their start and end apart: 5, of which 5 were waited for; matrix products, arithmetic and copies ran while one was open for 3% of the time, Pallas kernels for 0%

commit v1 on v0

--- a/solution.py
+++ b/solution.py
@@ -1,6 +1,10 @@
+import functools
+
 import jax
 import jax.numpy as jnp
 from jax import lax
+from jax.experimental import pallas as pl
+from jax.experimental.pallas import tpu as pltpu
 from jax.sharding import PartitionSpec as P
 
 K4 = 64
@@ -102,10 +106,418 @@
     return (fine_out, middle_out.astype(jnp.bfloat16), third_out.astype(jnp.bfloat16), spread)
 
 
+LANES = 128
+BF = jnp.bfloat16
+F32 = jnp.float32
+MESH = pl.DeviceIdType.MESH
+
+
+def rows_hot(size, ids):
+    shape = (size, ids.shape[1])
+    return jnp.where(lax.broadcasted_iota(jnp.int32, shape, 0) == ids, 1.0, 0.0).astype(BF)
+
+
+def column_of(ids):
+    return jnp.broadcast_to(ids.astype(F32), (LANES, ids.shape[1])).T
+
+
+def lanes_hot(column, start):
+    lane = lax.broadcasted_iota(jnp.int32, column.shape, 1).astype(F32) + float(start)
+    return jnp.where(column == lane, 1.0, 0.0).astype(BF)
+
+
+def dot(a, b):
+    return jnp.dot(a, b, preferred_element_type=F32)
+
+
+def pieces(x, count):
+    out = []
+    for _ in range(count):
+        part = x.astype(BF)
+        out.append(part)
+        x = x - part.astype(F32)
+    return out
+
+
+def dot_left(x, hot, count=3):
+    return sum(dot(part, hot) for part in pieces(x, count))
+
+
+def widen(column, width):
+    return jnp.concatenate([column] * (width // LANES), axis=1)
+
+
+def sweep(
+    n,
+    m,
+    fa_ref,
+    p1_ref,
+    p2_ref,
+    p3_ref,
+    shrink_ref,
+    rows_ref,
+    fine_ref,
+    mid_ref,
+    coarse_ref,
+    spread_ref,
+    fa_all,
+    p1_all,
+    got,
+    h1f,
+    h2f,
+    h3f,
+    h1r,
+    h1m,
+    h23,
+    sums1,
+    sums2,
+    part_own,
+    part_all,
+    cnt_own,
+    cnt_all,
+    means3,
+    fine_own,
+    mid_own,
+    coarse_own,
+    err_own,
+    err_all,
+    tally,
+    id_send,
+    id_recv,
+    row_send,
+    row_recv,
+    part_send,
+    part_recv,
+    cnt_send,
+    cnt_recv,
+    back_send,
+    back_recv,
+    out_send,
+    out_recv,
+    local_sem,
+):
+    me = lax.axis_index("clus")
+    dp = lax.axis_index("dp")
+    count, width = rows_ref.shape
+    share = width // n
+    fine_dev = p1_ref.shape[1]
+    middle = p2_ref.shape[1]
+    third = p3_ref.shape[1]
+    devices = n * m
+    total = count * devices
+    fine = n * fine_dev
+    thin = share // m
+    mid_share = middle // n
+    third_share = third // devices
+    w4 = shrink_ref[0] * (total / K4)
+    w3 = shrink_ref[1] * (total / third)
+    w2 = shrink_ref[2] * (total / (middle * m))
+    w1 = shrink_ref[3] * (total / (fine_dev * devices))
+
+    def span(index, size):
+        return pl.ds(pl.multiple_of(index * size, size), size)
+
+    def to_clus(k, src, dst, send, recv):
+        return pltpu.make_async_remote_copy(
+            src_ref=src,
+            dst_ref=dst,
+            send_sem=send,
+            recv_sem=recv,
+            device_id={"clus": lax.rem(me + k, n)},
+            device_id_type=MESH,
+        )
+
+    def to_dp(k, src, dst, send, recv):
+        return pltpu.make_async_remote_copy(
+            src_ref=src,
+            dst_ref=dst,
+            send_sem=send,
+            recv_sem=recv,
+            device_id={"dp": lax.rem(dp + k, m)},
+            device_id_type=MESH,
+        )
+
+    barrier = pltpu.get_barrier_semaphore()
+    for k in range(1, n):
+        pl.semaphore_signal(
+            barrier, inc=1, device_id={"clus": lax.rem(me + k, n)}, device_id_type=MESH
+        )
+    for k in range(1, m):
+        pl.semaphore_signal(
+            barrier, inc=1, device_id={"dp": lax.rem(dp + k, m)}, device_id_type=MESH
+        )
+    own_rows = pltpu.make_async_copy(
+        rows_ref.at[:, span(me, share)], got.at[span(me, count), :], local_sem.at[0]
+    )
+    own_rows.start()
+    fa_all[me] = fa_ref[...]
+    p1_all[me] = p1_ref[...]
+    pl.semaphore_wait(barrier, n - 1 + m - 1)
+
+    id_copies = []
+    row_copies = []
+    for k in range(1, n):
+        id_copies.append(to_clus(k, fa_ref, fa_all.at[me], id_send.at[0, k], id_recv.at[0, k]))
+        id_copies.append(to_clus(k, p1_ref, p1_all.at[me], id_send.at[1, k], id_recv.at[1, k]))
+    for copy in id_copies:
+        copy.start()
+    for k in range(1, n):
+        peer = lax.rem(me + k, n)
+        copy = to_clus(
+            k,
+            rows_ref.at[:, span(peer, share)],
+            got.at[span(me, count), :],
+            row_send.at[k],
+            row_recv.at[k],
+        )
+        copy.start()
+        row_copies.append(copy)
+
+    p2_row = p2_ref[...]
+    p3_row = p3_ref[...]
+    h23[...] = rows_hot(third, p2_row)
+    h4 = lanes_hot(column_of(p3_row), 0)
+    h4f = rows_hot(LANES, p3_row)
+    high = p2_row // 256
+    top_line = lax.broadcasted_iota(jnp.int32, (16, middle), 0) == 0
+    p2_split = jnp.where(top_line, high, p2_row - high * 256).astype(F32).astype(BF)
+
+    for copy in id_copies:
+        copy.wait_recv()
+    fa_row = jnp.concatenate([fa_all[i] for i in range(n)], axis=1) - dp * fine
+    p1_row = jnp.concatenate([p1_all[i] for i in range(n)], axis=1) - dp * middle
+    h1f[...] = rows_hot(fine, fa_row)
+    p1_lines = jnp.broadcast_to(p1_row, (16, fine)).astype(F32).astype(BF)
+    mid_row = dot(p1_lines, h1f[...])[0:1].astype(jnp.int32)
+    h2f[...] = rows_hot(middle, mid_row)
+    halves = dot(p2_split, h2f[...])
+    third_row = (halves[0:1] * 256.0 + halves[1:2]).astype(jnp.int32)
+    h3f[...] = rows_hot(third, third_row)
+    ones = jnp.ones((n * count, LANES), BF)
+    cnt_part = dot(h3f[...], ones).T[0:1]
+    cnt_own[...] = cnt_part
+    cnt_all[dp] = cnt_part
+    dp_copies = []
+    for k in range(1, m):
+        copy = to_dp(k, cnt_own, cnt_all.at[dp], cnt_send.at[k], cnt_recv.at[k])
+        copy.start()
+        dp_copies.append(copy)
+
+    own_rows.wait()
+    for copy in row_copies:
+        copy.wait_recv()
+    part_own[...] = dot(h3f[...], got[...]).T
+    for k in range(1, m):
+        peer = lax.rem(dp + k, m)
+        copy = to_dp(
+            k, part_own.at[span(peer, thin), :], part_all.at[dp], part_send.at[k], part_recv.at[k]
+        )
+        copy.start()
+        dp_copies.append(copy)
+
+    sums1[...] = dot(h1f[...], got[...])
+    sums2[...] = dot(h2f[...], got[...])
+    scale1 = 1.0 / (dot(h1f[...], ones) + w1)
+    scale2 = 1.0 / (dot(h2f[...], ones) + w2)
+    fa_column = column_of(fa_row)
+    for j in range(0, fine, LANES):
+        h1r[:, j : j + LANES] = lanes_hot(fa_column, j)
+    p1_column = column_of(p1_row)
+    for j in range(0, middle, LANES):
+        h1m[:, j : j + LANES] = lanes_hot(p1_column, j)
+    part_all[dp] = part_own[span(dp, thin), :]
+
+    for copy in dp_copies:
+        copy.wait_recv()
+    sums3 = part_all[0]
+    cnt3 = cnt_all[0]
+    for i in range(1, m):
+        sums3 = sums3 + part_all[i]
+        cnt3 = cnt3 + cnt_all[i]
+    sums4 = dot_left(sums3, h4)
+    cnt4 = dot_left(jnp.broadcast_to(cnt3, (16, third)), h4)[0:1]
+    center = jnp.sum(sums4, axis=1, keepdims=True) / total
+    means4 = (sums4 + w4 * center) / (cnt4 + w4)
+    means3[dp] = ((sums3 + w3 * dot_left(means4, h4f)) / (cnt3 + w3)).astype(BF)
+    back_copies = []
+    for k in range(1, m):
+        copy = to_dp(k, means3.at[dp], means3.at[dp], back_send.at[k], back_recv.at[k])
+        copy.start()
+        back_copies.append(copy)
+    for copy in back_copies:
+        copy.wait_recv()
+
+    means3_all = means3[...].reshape(share, third)
+    prior2 = dot(means3_all, h23[...]).T
+    means2 = (sums2[...] + w2 * prior2) * widen(scale2, share)
+    prior1 = sum(dot(h1m[...], part) for part in pieces(means2, 2))
+    fine_own[...] = ((sums1[...] + w1 * prior1) * widen(scale1, share)).astype(BF)
+    mid_own[...] = means2.astype(BF)
+    coarse_own[...] = means3_all.astype(F32).T.astype(BF)
+    columns = span(me, share)
+    out_copies = []
+    local_copies = []
+    plan = (
+        (fine_own, fine_ref, lambda peer: span(peer, fine_dev)),
+        (mid_own, mid_ref, lambda peer: span(peer, mid_share)),
+        (coarse_own, coarse_ref, lambda peer: span(dp * n + peer, third_share)),
+    )
+    for which, (src, dst, place) in enumerate(plan):
+        for k in range(1, n):
+            peer = lax.rem(me + k, n)
+            copy = to_clus(
+                k,
+                src.at[place(peer), :],
+                dst.at[:, columns],
+                out_send.at[which, k],
+                out_recv.at[which, k],
+            )
+            copy.start()
+            out_copies.append(copy)
+        copy = pltpu.make_async_copy(
+            src.at[place(me), :], dst.at[:, columns], local_sem.at[1 + which]
+        )
+        copy.start()
+        local_copies.append(copy)
+
+    diff = got[...].astype(F32) - dot(h1r[...], fine_own[...])
+    square = diff * diff
+    folded = square[:, :LANES]
+    for j in range(LANES, share, LANES):
+        folded = folded + square[:, j : j + LANES]
+    err_row = jnp.sum(folded.T, axis=0, keepdims=True)
+    parts = pieces(err_row, 3)
+    line = lax.broadcasted_iota(jnp.int32, (16, n * count), 0)
+    stack = jnp.where(line == 3, 1.0, 0.0)
+    for i, part in enumerate(parts):
+        stack = jnp.where(line == i, part.astype(F32), stack)
+    by_fine = dot(stack.astype(BF), h1r[...])
+    err_fine = by_fine[0:1] + by_fine[1:2] + by_fine[2:3]
+    for i in range(n):
+        err_own[i] = err_fine[:, i * fine_dev : (i + 1) * fine_dev]
+        tally[i] = by_fine[3:4, i * fine_dev : (i + 1) * fine_dev]
+    err_copies = []
+    for k in range(1, n):
+        peer = lax.rem(me + k, n)
+        copy = to_clus(k, err_own.at[peer], err_all.at[me], out_send.at[3, k], out_recv.at[3, k])
+        copy.start()
+        err_copies.append(copy)
+    err_all[me] = err_own[me]
+    for copy in err_copies:
+        copy.wait_recv()
+    err = err_all[0]
+    for i in range(1, n):
+        err = err + err_all[i]
+    spread_ref[...] = err / (width * (tally[me] + 1.0))
+    for copy in local_copies:
+        copy.wait()
+    for copy in out_copies:
+        copy.wait_recv()
+    for copy in id_copies + row_copies + dp_copies + back_copies + out_copies + err_copies:
+        copy.wait_send()
+
+
+def fused(rows, fine_assign, parent1, parent2, parent3, shrink):
+    n = lax.axis_size("clus")
+    m = lax.axis_size("dp")
+    count, width = rows.shape
+    fine_dev = parent1.shape[0]
+    middle = parent2.shape[0]
+    third = parent3.shape[0]
+    share = width // n
+    thin = share // m
+    fine = n * fine_dev
+    total_rows = n * count
+    vmem = pl.BlockSpec(memory_space=pltpu.VMEM)
+    dma = pltpu.SemaphoreType.DMA
+    fine_out, mid_out, coarse_out, spread = pl.pallas_call(
+        functools.partial(sweep, n, m),
+        out_shape=(
+            jax.ShapeDtypeStruct((fine_dev, width), BF),
+            jax.ShapeDtypeStruct((middle // n, width), BF),
+            jax.ShapeDtypeStruct((third // (n * m), width), BF),
+            jax.ShapeDtypeStruct((1, fine_dev), F32),
+        ),
+        in_specs=[vmem] * 4
+        + [pl.BlockSpec(memory_space=pltpu.SMEM), pl.BlockSpec(memory_space=pl.ANY)],
+        out_specs=[vmem] * 4,
+        scratch_shapes=[
+            pltpu.VMEM((n, 1, count), jnp.int32),
+            pltpu.VMEM((n, 1, fine_dev), jnp.int32),
+            pltpu.VMEM((total_rows, share), BF),
+            pltpu.VMEM((fine, total_rows), BF),
+            pltpu.VMEM((middle, total_rows), BF),
+            pltpu.VMEM((third, total_rows), BF),
+            pltpu.VMEM((total_rows, fine), BF),
+            pltpu.VMEM((fine, middle), BF),
+            pltpu.VMEM((third, middle), BF),
+            pltpu.VMEM((fine, share), F32),
+            pltpu.VMEM((middle, share), F32),
+            pltpu.VMEM((share, third), F32),
+            pltpu.VMEM((m, thin, third), F32),
+            pltpu.VMEM((1, third), F32),
+            pltpu.VMEM((m, 1, third), F32),
+            pltpu.VMEM((m, thin, third), BF),
+            pltpu.VMEM((fine, share), BF),
+            pltpu.VMEM((middle, share), BF),
+            pltpu.VMEM((third, share), BF),
+            pltpu.VMEM((n, 1, fine_dev), F32),
+            pltpu.VMEM((n, 1, fine_dev), F32),
+            pltpu.VMEM((n, 1, fine_dev), F32),
+            dma((2, n)),
+            dma((2, n)),
+            dma((n,)),
+            dma((n,)),
+            dma((m,)),
+            dma((m,)),
+            dma((m,)),
+            dma((m,)),
+            dma((m,)),
+            dma((m,)),
+            dma((4, n)),
+            dma((4, n)),
+            dma((4,)),
+        ],
+        compiler_params=pltpu.CompilerParams(
+            collective_id=0, has_side_effects=True, vmem_limit_bytes=60 << 20
+        ),
+        name="sweep",
+    )(
+        fine_assign.reshape(1, count),
+        parent1.reshape(1, fine_dev),
+        parent2.reshape(1, middle),
+        parent3.reshape(1, third),
+        shrink,
+        rows,
+    )
+    return fine_out, mid_out, coarse_out, spread.reshape(fine_dev)
+
+
+def fits(rows, fine_assign, parent1, parent2, parent3):
+    n = lax.axis_size("clus")
+    m = lax.axis_size("dp")
+    return (
+        rows.shape[1] % (n * LANES) == 0
+        and (rows.shape[1] // n) % (m * 16) == 0
+        and rows.shape[0] % LANES == 0
+        and parent1.shape[0] % LANES == 0
+        and parent2.shape[0] % LANES == 0
+        and parent2.shape[0] <= 256
+        and parent2.shape[0] % (n * 16) == 0
+        and parent3.shape[0] % LANES == 0
+        and parent3.shape[0] % (n * m * 16) == 0
+    )
+
+
+def step(rows, fine_assign, parent1, parent2, parent3, shrink):
+    form = fused if fits(rows, fine_assign, parent1, parent2, parent3) else local
+    return form(rows, fine_assign, parent1, parent2, parent3, shrink)
+
+
 def solution(mesh):
     placed = (P(("dp", "clus"), None), P(("dp", "clus")), P(("dp", "clus")), P("dp"), P(), P())
     return jax.shard_map(
-        local,
+        step,
         mesh=mesh,
         in_specs=placed,
         out_specs=(

time: 254 us -> 49.8 us (0.20)
  waiting for transfers between devices: 149 us -> 0 us
  blocking collectives: 48.4 us -> 0 us
  Pallas kernels: 0 us -> 45 us
  between operations: 17.3 us -> 0.65 us
  matrix products: 15.1 us -> 0 us
  local copies, waits for them, and re-layouts: 13 us -> 3.89 us
  starting transfers between devices: 8.83 us -> 0 us
    psum x1 -> x0, waiting for transfers between devices: 87.8 us -> none  [local(): lax.psum((third_part, third_tally), ('dp', 'clus'))]
    pallas_call x0 -> x1, Pallas kernels: none -> 45 us  [fused(): pl.pallas_call(functools.partial(sweep, n, m), out_shape=(jax.ShapeDtypeS...]
    psum x1 -> x0, blocking collectives: 39.4 us -> none  [local(): lax.psum((third_part, third_tally), ('dp', 'clus'))]
    reduce_scatter x1 -> x0, waiting for transfers between devices: 23.7 us -> none  [local(): lax.psum_scatter(middle_part, 'clus', scatter_dimension=0, tiled=True)]
    all_gather x1 -> x0, waiting for transfers between devices: 23.3 us -> none  [local(): middle_means = lax.all_gather(middle_out, 'clus', axis=0, tiled=True)]
    dot_general x12 -> x0, matrix products: 15.1 us -> none  [the longest x1 3.23 us: local(): third_part = jnp.dot(third_hot, middle_sums, precision=HIGH)]
    all_to_all x2 -> x0, waiting for transfers between devices: 14.1 us -> none  [the longest x1 12.4 us: local(): lax.all_to_all(send_rows, 'clus', split_axis=0, concat_axis=0, tiled=True)]
    unnamed x1 -> x0, blocking collectives: 8.99 us -> none
  transfers between devices with their start and end apart: 5 -> 0, of which waited for: 5 -> 0; matrix products, arithmetic and copies ran while one was open for 3% -> 0% of each run, Pallas kernels for 0% -> 0%
where the time goes in v1:
time: 49.8 us; the launch traced here: 49.6 us
  Pallas kernels  45 us (90%)
  local copies, waits for them, and re-layouts  3.89 us (8%)
  between operations  0.65 us (1%)
    pallas_call x1, Pallas kernels, fused(): pl.pallas_call(functools.partial(sweep, n, m), out_shape=(jax.ShapeDtypeS...  45 us
    unnamed x10, local copies, waits for them, and re-layouts  3.89 us

profile of v1, /device:TPU:0, one launch (start us, length us, event | category | flops | bytes accessed | tf_op | source)
XLA Modules:
  0.0 49.6 jit_solution(15986601610085269114)
XLA Ops:
  0.6 45.0 %sweep.1 = (bf16[256,1024]{1,0:T(8,128)(2,1)}, bf16[64,1024]{1,0:T(8,128)(2,1)}, bf16[16,1024]{1,0:T(8,128)(2,1)}, f32[1,256]{1,0:T(1,128)}) custom-call(s32[1,256]{1,0:T(1,128)} %bitcast.6, s32[1,256]{1,0:T(1,128)} %bitcast.7, s32[1,256]{1,0:T(1,128)} %bitcast.8, s32[1,512]{1,0:T(1,128)} %bitcast.5, f32[4]{0:T(128)} %shrink_ref.1, bf16[256,1024]{1,0:T(8,128)(2,1)} %rows_ref.1), custom_call_target="tpu_custom_call" | custom-call | tf_op jit(solution)/shard_map/sweep/pallas_call | solution.py:433
  45.7 0.0 copy-start
  45.7 1.9 %copy.14 = bf16[256,1024]{1,0:T(8,128)(2,1)} copy(bf16[256,1024]{1,0:T(8,128)(2,1)} %get-tuple-element.16) | data formatting | bytes 1048576
  47.6 0.0 copy-done
  47.6 0.0 copy-start.1
  47.6 0.7 %copy.15 = bf16[64,1024]{1,0:T(8,128)(2,1)} copy(bf16[64,1024]{1,0:T(8,128)(2,1)S(1)} %copy-done) | data formatting | bytes 262144
  48.3 0.1 copy-done.1
  48.4 0.0 copy-start.2
  48.4 0.6 %copy.16 = bf16[16,1024]{1,0:T(8,128)(2,1)} copy(bf16[16,1024]{1,0:T(8,128)(2,1)S(1)} %copy-done.1) | data formatting | bytes 65536
  49.0 0.0 copy-done.2
  49.0 0.6 %copy.17 = f32[256]{0:T(256)} copy(f32[256]{0:T(256)S(1)} %bitcast.9) | data formatting | bytes 2048
Async XLA Ops:
  45.7 1.9 %copy-start = (bf16[64,1024]{1,0:T(8,128)(2,1)S(1)}, bf16[64,1024]{1,0:T(8,128)(2,1)}, u32[]{:S(2)}) copy-start(bf16[64,1024]{1,0:T(8,128)(2,1)} %get-tuple-element.17) | copy-start | bytes 393220
  47.6 0.8 %copy-start.1 = (bf16[16,1024]{1,0:T(8,128)(2,1)S(1)}, bf16[16,1024]{1,0:T(8,128)(2,1)}, u32[]{:S(2)}) copy-start(bf16[16,1024]{1,0:T(8,128)(2,1)} %get-tuple-element.18) | copy-start | bytes 98308
  48.4 0.7 %copy-start.2 = (f32[1,256]{1,0:T(1,128)S(1)}, f32[1,256]{1,0:T(1,128)}, u32[]{:S(2)}) copy-start(f32[1,256]{1,0:T(1,128)} %get-tuple-element.11) | copy-start | bytes 3076

commit v2 on v1

--- a/solution.py
+++ b/solution.py
@@ -143,10 +143,6 @@
     return sum(dot(part, hot) for part in pieces(x, count))
 
 
-def widen(column, width):
-    return jnp.concatenate([column] * (width // LANES), axis=1)
-
-
 def sweep(
     n,
     m,
@@ -169,9 +165,13 @@
     h1r,
     h1m,
     h23,
-    sums1,
-    sums2,
+    base1,
+    base2,
+    pull1,
+    pull2,
     part_own,
+    pair_got,
+    pair_sum,
     part_all,
     cnt_own,
     cnt_all,
@@ -186,12 +186,18 @@
     id_recv,
     row_send,
     row_recv,
+    pair_send,
+    pair_recv,
     part_send,
     part_recv,
     cnt_send,
     cnt_recv,
     back_send,
     back_recv,
+    relay_send,
+    relay_recv,
+    fine_send,
+    fine_recv,
     out_send,
     out_recv,
     local_sem,
@@ -200,13 +206,18 @@
     dp = lax.axis_index("dp")
     count, width = rows_ref.shape
     share = width // n
+    chunks = share // LANES
     fine_dev = p1_ref.shape[1]
     middle = p2_ref.shape[1]
     third = p3_ref.shape[1]
     devices = n * m
     total = count * devices
     fine = n * fine_dev
-    thin = share // m
+    pairs = m // 2
+    half = LANES // 2
+    thin = half // pairs
+    pair = dp // 2
+    side = lax.rem(dp, 2)
     mid_share = middle // n
     third_share = third // devices
     w4 = shrink_ref[0] * (total / K4)
@@ -217,64 +228,80 @@
     def span(index, size):
         return pl.ds(pl.multiple_of(index * size, size), size)
 
-    def to_clus(k, src, dst, send, recv):
+    def chunk_of(h):
+        return slice(h * LANES, (h + 1) * LANES)
+
+    def remote(src, dst, send, recv, device):
         return pltpu.make_async_remote_copy(
             src_ref=src,
             dst_ref=dst,
             send_sem=send,
             recv_sem=recv,
-            device_id={"clus": lax.rem(me + k, n)},
+            device_id=device,
             device_id_type=MESH,
         )
 
-    def to_dp(k, src, dst, send, recv):
-        return pltpu.make_async_remote_copy(
-            src_ref=src,
-            dst_ref=dst,
-            send_sem=send,
-            recv_sem=recv,
-            device_id={"dp": lax.rem(dp + k, m)},
-            device_id_type=MESH,
-        )
+    def clus_peer(k):
+        return {"clus": lax.rem(me + k, n)}
+
+    def dp_peer(k):
+        return {"dp": lax.rem(dp + k, m)}
+
+    def pair_peer(k):
+        return {"dp": lax.rem(pair + k, pairs) * 2 + side}
+
+    other = {"dp": pair * 2 + 1 - side}
+
+    started = []
+
+    def start(copies):
+        for copy in copies:
+            copy.start()
+        started.extend(copies)
+        return copies
+
+    def arrive(copies):
+        for copy in copies:
+            copy.wait_recv()
 
     barrier = pltpu.get_barrier_semaphore()
     for k in range(1, n):
-        pl.semaphore_signal(
-            barrier, inc=1, device_id={"clus": lax.rem(me + k, n)}, device_id_type=MESH
-        )
+        pl.semaphore_signal(barrier, inc=1, device_id=clus_peer(k), device_id_type=MESH)
     for k in range(1, m):
-        pl.semaphore_signal(
-            barrier, inc=1, device_id={"dp": lax.rem(dp + k, m)}, device_id_type=MESH
-        )
+        pl.semaphore_signal(barrier, inc=1, device_id=dp_peer(k), device_id_type=MESH)
     own_rows = pltpu.make_async_copy(
         rows_ref.at[:, span(me, share)], got.at[span(me, count), :], local_sem.at[0]
     )
     own_rows.start()
     fa_all[me] = fa_ref[...]
     p1_all[me] = p1_ref[...]
-    pl.semaphore_wait(barrier, n - 1 + m - 1)
-
-    id_copies = []
-    row_copies = []
-    for k in range(1, n):
-        id_copies.append(to_clus(k, fa_ref, fa_all.at[me], id_send.at[0, k], id_recv.at[0, k]))
-        id_copies.append(to_clus(k, p1_ref, p1_all.at[me], id_send.at[1, k], id_recv.at[1, k]))
-    for copy in id_copies:
-        copy.start()
-    for k in range(1, n):
-        peer = lax.rem(me + k, n)
-        copy = to_clus(
-            k,
-            rows_ref.at[:, span(peer, share)],
-            got.at[span(me, count), :],
-            row_send.at[k],
-            row_recv.at[k],
-        )
-        copy.start()
-        row_copies.append(copy)
-
     p2_row = p2_ref[...]
     p3_row = p3_ref[...]
+    pl.semaphore_wait(barrier, n - 1 + m - 1)
+
+    id_copies = []
+    for k in range(1, n):
+        for which, (src, dst) in enumerate(((fa_ref, fa_all), (p1_ref, p1_all))):
+            id_copies.append(
+                remote(src, dst.at[me], id_send.at[which, k], id_recv.at[which, k], clus_peer(k))
+            )
+    start(id_copies)
+    row_copies = []
+    for h in range(chunks):
+        copies = []
+        for k in range(1, n):
+            column = lax.rem(me + k, n) * share + h * LANES
+            copies.append(
+                remote(
+                    rows_ref.at[:, pl.ds(pl.multiple_of(column, LANES), LANES)],
+                    got.at[span(me, count), chunk_of(h)],
+                    row_send.at[h, k],
+                    row_recv.at[h, k],
+                    clus_peer(k),
+                )
+            )
+        row_copies.append(start(copies))
+
     h23[...] = rows_hot(third, p2_row)
     h4 = lanes_hot(column_of(p3_row), 0)
     h4f = rows_hot(LANES, p3_row)
@@ -282,8 +309,7 @@
     top_line = lax.broadcasted_iota(jnp.int32, (16, middle), 0) == 0
     p2_split = jnp.where(top_line, high, p2_row - high * 256).astype(F32).astype(BF)
 
-    for copy in id_copies:
-        copy.wait_recv()
+    arrive(id_copies)
     fa_row = jnp.concatenate([fa_all[i] for i in range(n)], axis=1) - dp * fine
     p1_row = jnp.concatenate([p1_all[i] for i in range(n)], axis=1) - dp * middle
     h1f[...] = rows_hot(fine, fa_row)
@@ -294,91 +320,143 @@
     third_row = (halves[0:1] * 256.0 + halves[1:2]).astype(jnp.int32)
     h3f[...] = rows_hot(third, third_row)
     ones = jnp.ones((n * count, LANES), BF)
+    own_rows.wait()
+
+    pair_copies = []
+    part_copies = []
+    back_copies = []
+    relay_copies = []
+    cnt_copies = []
+
+    def sum_part(h):
+        arrive(row_copies[h])
+        part_own[h] = dot(h3f[...], got[:, chunk_of(h)]).T
+        away = part_own.at[h, span(1 - side, half), :]
+        copy = remote(away, pair_got.at[h], pair_send.at[h], pair_recv.at[h], other)
+        pair_copies.append(start([copy]))
+
+    def sum_pair(h):
+        arrive(pair_copies[h])
+        pair_sum[h] = part_own[h, span(side, half), :] + pair_got[h]
+        copies = []
+        for k in range(1, pairs):
+            copies.append(
+                remote(
+                    pair_sum.at[h, span(lax.rem(pair + k, pairs), thin), :],
+                    part_all.at[h, pair],
+                    part_send.at[h, k],
+                    part_recv.at[h, k],
+                    pair_peer(k),
+                )
+            )
+        part_copies.append(start(copies))
+        part_all[h, pair] = pair_sum[h, span(pair, thin), :]
+
+    def third_level(h, cnt3, cnt4):
+        arrive(part_copies[h])
+        sums3 = part_all[h, 0]
+        for i in range(1, pairs):
+            sums3 = sums3 + part_all[h, i]
+        sums4 = dot_left(sums3, h4)
+        center = jnp.sum(sums4, axis=1, keepdims=True) / total
+        means4 = (sums4 + w4 * center) / (cnt4 + w4)
+        place = span(side * pairs + pair, thin)
+        means3[h, place, :] = ((sums3 + w3 * dot_left(means4, h4f)) / (cnt3 + w3)).astype(BF)
+        copies = []
+        for k in range(1, pairs):
+            block = means3.at[h, place, :]
+            copies.append(remote(block, block, back_send.at[h, k], back_recv.at[h, k], pair_peer(k)))
+        back_copies.append(start(copies))
+
+    def relay(h):
+        arrive(back_copies[h])
+        block = means3.at[h, span(side, half), :]
+        copy = remote(block, block, relay_send.at[h], relay_recv.at[h], other)
+        relay_copies.append(start([copy]))
+
+    sum_part(0)
     cnt_part = dot(h3f[...], ones).T[0:1]
     cnt_own[...] = cnt_part
     cnt_all[dp] = cnt_part
-    dp_copies = []
     for k in range(1, m):
-        copy = to_dp(k, cnt_own, cnt_all.at[dp], cnt_send.at[k], cnt_recv.at[k])
-        copy.start()
-        dp_copies.append(copy)
-
-    own_rows.wait()
-    for copy in row_copies:
-        copy.wait_recv()
-    part_own[...] = dot(h3f[...], got[...]).T
-    for k in range(1, m):
-        peer = lax.rem(dp + k, m)
-        copy = to_dp(
-            k, part_own.at[span(peer, thin), :], part_all.at[dp], part_send.at[k], part_recv.at[k]
+        cnt_copies.append(
+            remote(cnt_own, cnt_all.at[dp], cnt_send.at[k], cnt_recv.at[k], dp_peer(k))
         )
-        copy.start()
-        dp_copies.append(copy)
-
-    sums1[...] = dot(h1f[...], got[...])
-    sums2[...] = dot(h2f[...], got[...])
+    start(cnt_copies)
+    p1_column = column_of(p1_row)
+    for j in range(0, middle, LANES):
+        h1m[:, j : j + LANES] = lanes_hot(p1_column, j)
+    for h in range(1, chunks):
+        sum_pair(h - 1)
+        sum_part(h)
     scale1 = 1.0 / (dot(h1f[...], ones) + w1)
     scale2 = 1.0 / (dot(h2f[...], ones) + w2)
+    pull1[...] = w1 * scale1
+    pull2[...] = w2 * scale2
+    sum_pair(chunks - 1)
+    for h in range(chunks):
+        base1[:, chunk_of(h)] = dot(h1f[...], got[:, chunk_of(h)]) * scale1
+        base2[:, chunk_of(h)] = dot(h2f[...], got[:, chunk_of(h)]) * scale2
+    arrive(cnt_copies)
+    cnt3 = cnt_all[0]
+    for i in range(1, m):
+        cnt3 = cnt3 + cnt_all[i]
+    cnt4 = dot_left(jnp.broadcast_to(cnt3, (16, third)), h4)[0:1]
+    for h in range(chunks):
+        third_level(h, cnt3, cnt4)
     fa_column = column_of(fa_row)
     for j in range(0, fine, LANES):
         h1r[:, j : j + LANES] = lanes_hot(fa_column, j)
-    p1_column = column_of(p1_row)
-    for j in range(0, middle, LANES):
-        h1m[:, j : j + LANES] = lanes_hot(p1_column, j)
-    part_all[dp] = part_own[span(dp, thin), :]
-
-    for copy in dp_copies:
-        copy.wait_recv()
-    sums3 = part_all[0]
-    cnt3 = cnt_all[0]
-    for i in range(1, m):
-        sums3 = sums3 + part_all[i]
-        cnt3 = cnt3 + cnt_all[i]
-    sums4 = dot_left(sums3, h4)
-    cnt4 = dot_left(jnp.broadcast_to(cnt3, (16, third)), h4)[0:1]
-    center = jnp.sum(sums4, axis=1, keepdims=True) / total
-    means4 = (sums4 + w4 * center) / (cnt4 + w4)
-    means3[dp] = ((sums3 + w3 * dot_left(means4, h4f)) / (cnt3 + w3)).astype(BF)
-    back_copies = []
-    for k in range(1, m):
-        copy = to_dp(k, means3.at[dp], means3.at[dp], back_send.at[k], back_recv.at[k])
-        copy.start()
-        back_copies.append(copy)
-    for copy in back_copies:
-        copy.wait_recv()
-
-    means3_all = means3[...].reshape(share, third)
-    prior2 = dot(means3_all, h23[...]).T
-    means2 = (sums2[...] + w2 * prior2) * widen(scale2, share)
-    prior1 = sum(dot(h1m[...], part) for part in pieces(means2, 2))
-    fine_own[...] = ((sums1[...] + w1 * prior1) * widen(scale1, share)).astype(BF)
-    mid_own[...] = means2.astype(BF)
-    coarse_own[...] = means3_all.astype(F32).T.astype(BF)
+    for h in range(chunks):
+        relay(h)
+
+    fine_copies = []
+    local_copies = []
+    for h in range(chunks):
+        arrive(relay_copies[h])
+        columns = pl.ds(pl.multiple_of(me * share + h * LANES, LANES), LANES)
+        means2 = base2[:, chunk_of(h)] + pull2[...] * dot(means3[h], h23[...]).T
+        mid_own[:, chunk_of(h)] = means2.astype(BF)
+        parts = pieces(means2, 2)
+        for k in (*range(1, n), 0):
+            block = span(lax.rem(me + k, n), fine_dev)
+            prior = sum(dot(h1m[block, :], part) for part in parts)
+            means1 = base1[block, chunk_of(h)] + pull1[block, :] * prior
+            fine_own[block, chunk_of(h)] = means1.astype(BF)
+            src = fine_own.at[block, chunk_of(h)]
+            dst = fine_ref.at[:, columns]
+            if k:
+                copy = remote(src, dst, fine_send.at[h, k], fine_recv.at[h, k], clus_peer(k))
+                fine_copies.extend(start([copy]))
+            else:
+                copy = pltpu.make_async_copy(src, dst, local_sem.at[3 + h])
+                copy.start()
+                local_copies.append(copy)
+    for h in range(chunks):
+        coarse_own[:, chunk_of(h)] = means3[h].astype(F32).T.astype(BF)
     columns = span(me, share)
     out_copies = []
-    local_copies = []
     plan = (
-        (fine_own, fine_ref, lambda peer: span(peer, fine_dev)),
         (mid_own, mid_ref, lambda peer: span(peer, mid_share)),
         (coarse_own, coarse_ref, lambda peer: span(dp * n + peer, third_share)),
     )
     for which, (src, dst, place) in enumerate(plan):
         for k in range(1, n):
-            peer = lax.rem(me + k, n)
-            copy = to_clus(
-                k,
-                src.at[place(peer), :],
-                dst.at[:, columns],
-                out_send.at[which, k],
-                out_recv.at[which, k],
+            out_copies.append(
+                remote(
+                    src.at[place(lax.rem(me + k, n)), :],
+                    dst.at[:, columns],
+                    out_send.at[which, k],
+                    out_recv.at[which, k],
+                    clus_peer(k),
+                )
             )
-            copy.start()
-            out_copies.append(copy)
         copy = pltpu.make_async_copy(
             src.at[place(me), :], dst.at[:, columns], local_sem.at[1 + which]
         )
         copy.start()
         local_copies.append(copy)
+    start(out_copies)
 
     diff = got[...].astype(F32) - dot(h1r[...], fine_own[...])
     square = diff * diff
@@ -398,22 +476,22 @@
         tally[i] = by_fine[3:4, i * fine_dev : (i + 1) * fine_dev]
     err_copies = []
     for k in range(1, n):
-        peer = lax.rem(me + k, n)
-        copy = to_clus(k, err_own.at[peer], err_all.at[me], out_send.at[3, k], out_recv.at[3, k])
-        copy.start()
-        err_copies.append(copy)
+        src = err_own.at[lax.rem(me + k, n)]
+        err_copies.append(
+            remote(src, err_all.at[me], out_send.at[2, k], out_recv.at[2, k], clus_peer(k))
+        )
+    start(err_copies)
     err_all[me] = err_own[me]
-    for copy in err_copies:
-        copy.wait_recv()
+    arrive(err_copies)
     err = err_all[0]
     for i in range(1, n):
         err = err + err_all[i]
     spread_ref[...] = err / (width * (tally[me] + 1.0))
     for copy in local_copies:
         copy.wait()
-    for copy in out_copies:
-        copy.wait_recv()
-    for copy in id_copies + row_copies + dp_copies + back_copies + out_copies + err_copies:
+    arrive(out_copies)
+    arrive(fine_copies)
+    for copy in started:
         copy.wait_send()
 
 
@@ -425,7 +503,10 @@
     middle = parent2.shape[0]
     third = parent3.shape[0]
     share = width // n
-    thin = share // m
+    chunks = share // LANES
+    pairs = m // 2
+    half = LANES // 2
+    thin = half // pairs
     fine = n * fine_dev
     total_rows = n * count
     vmem = pl.BlockSpec(memory_space=pltpu.VMEM)
@@ -453,11 +534,15 @@
             pltpu.VMEM((third, middle), BF),
             pltpu.VMEM((fine, share), F32),
             pltpu.VMEM((middle, share), F32),
-            pltpu.VMEM((share, third), F32),
-            pltpu.VMEM((m, thin, third), F32),
+            pltpu.VMEM((fine, LANES), F32),
+            pltpu.VMEM((middle, LANES), F32),
+            pltpu.VMEM((chunks, LANES, third), F32),
+            pltpu.VMEM((chunks, half, third), F32),
+            pltpu.VMEM((chunks, half, third), F32),
+            pltpu.VMEM((chunks, pairs, thin, third), F32),
             pltpu.VMEM((1, third), F32),
             pltpu.VMEM((m, 1, third), F32),
-            pltpu.VMEM((m, thin, third), BF),
+            pltpu.VMEM((chunks, LANES, third), BF),
             pltpu.VMEM((fine, share), BF),
             pltpu.VMEM((middle, share), BF),
             pltpu.VMEM((third, share), BF),
@@ -466,17 +551,23 @@
             pltpu.VMEM((n, 1, fine_dev), F32),
             dma((2, n)),
             dma((2, n)),
-            dma((n,)),
-            dma((n,)),
+            dma((chunks, n)),
+            dma((chunks, n)),
+            dma((chunks,)),
+            dma((chunks,)),
+            dma((chunks, pairs)),
+            dma((chunks, pairs)),
             dma((m,)),
             dma((m,)),
-            dma((m,)),
-            dma((m,)),
-            dma((m,)),
-            dma((m,)),
-            dma((4, n)),
-            dma((4, n)),
-            dma((4,)),
+            dma((chunks, pairs)),
+            dma((chunks, pairs)),
+            dma((chunks,)),
+            dma((chunks,)),
+            dma((chunks, n)),
+            dma((chunks, n)),
+            dma((3, n)),
+            dma((3, n)),
+            dma((3 + chunks,)),
         ],
         compiler_params=pltpu.CompilerParams(
             collective_id=0, has_side_effects=True, vmem_limit_bytes=60 << 20
@@ -498,7 +589,8 @@
     m = lax.axis_size("dp")
     return (
         rows.shape[1] % (n * LANES) == 0
-        and (rows.shape[1] // n) % (m * 16) == 0
+        and m % 2 == 0
+        and (LANES // 2) % (m // 2 * 16) == 0
         and rows.shape[0] % LANES == 0
         and parent1.shape[0] % LANES == 0
         and parent2.shape[0] % LANES == 0

time: 49.8 us -> 42.3 us (0.85)
  Pallas kernels: 45 us -> 37.5 us
    pallas_call x1, Pallas kernels: 45 us -> 37.5 us  [fused(): pl.pallas_call(functools.partial(sweep, n, m), out_shape=(jax.ShapeDtypeS...]
where the time goes in v2:
time: 42.3 us; the launch traced here: 42 us
  Pallas kernels  37.5 us (89%)
  local copies, waits for them, and re-layouts  3.89 us (9%)
  between operations  0.65 us (2%)
    pallas_call x1, Pallas kernels, fused(): pl.pallas_call(functools.partial(sweep, n, m), out_shape=(jax.ShapeDtypeS...  37.5 us
    unnamed x10, local copies, waits for them, and re-layouts  3.89 us

profile of v2, /device:TPU:0, one launch (start us, length us, event | category | flops | bytes accessed | tf_op | source)
XLA Modules:
  0.0 42.0 jit_solution(16246784157170604783)
XLA Ops:
  0.6 37.5 %sweep.1 = (bf16[256,1024]{1,0:T(8,128)(2,1)}, bf16[64,1024]{1,0:T(8,128)(2,1)}, bf16[16,1024]{1,0:T(8,128)(2,1)}, f32[1,256]{1,0:T(1,128)}) custom-call(s32[1,256]{1,0:T(1,128)} %bitcast.6, s32[1,256]{1,0:T(1,128)} %bitcast.7, s32[1,256]{1,0:T(1,128)} %bitcast.8, s32[1,512]{1,0:T(1,128)} %bitcast.5, f32[4]{0:T(128)} %shrink_ref.1, bf16[256,1024]{1,0:T(8,128)(2,1)} %rows_ref.1), custom_call_target="tpu_custom_call" | custom-call | tf_op jit(solution)/shard_map/sweep/pallas_call | solution.py:514
  38.1 0.0 copy-start
  38.1 1.9 %copy.14 = bf16[256,1024]{1,0:T(8,128)(2,1)} copy(bf16[256,1024]{1,0:T(8,128)(2,1)} %get-tuple-element.16) | data formatting | bytes 1048576
  40.0 0.0 copy-done
  40.0 0.0 copy-start.1
  40.0 0.7 %copy.15 = bf16[64,1024]{1,0:T(8,128)(2,1)} copy(bf16[64,1024]{1,0:T(8,128)(2,1)S(1)} %copy-done) | data formatting | bytes 262144
  40.7 0.1 copy-done.1
  40.8 0.0 copy-start.2
  40.8 0.6 %copy.16 = bf16[16,1024]{1,0:T(8,128)(2,1)} copy(bf16[16,1024]{1,0:T(8,128)(2,1)S(1)} %copy-done.1) | data formatting | bytes 65536
  41.4 0.0 copy-done.2
  41.5 0.6 %copy.17 = f32[256]{0:T(256)} copy(f32[256]{0:T(256)S(1)} %bitcast.9) | data formatting | bytes 2048
Async XLA Ops:
  38.1 1.9 %copy-start = (bf16[64,1024]{1,0:T(8,128)(2,1)S(1)}, bf16[64,1024]{1,0:T(8,128)(2,1)}, u32[]{:S(2)}) copy-start(bf16[64,1024]{1,0:T(8,128)(2,1)} %get-tuple-element.17) | copy-start | bytes 393220
  40.0 0.8 %copy-start.1 = (bf16[16,1024]{1,0:T(8,128)(2,1)S(1)}, bf16[16,1024]{1,0:T(8,128)(2,1)}, u32[]{:S(2)}) copy-start(bf16[16,1024]{1,0:T(8,128)(2,1)} %get-tuple-element.18) | copy-start | bytes 98308
  40.8 0.7 %copy-start.2 = (f32[1,256]{1,0:T(1,128)S(1)}, f32[1,256]{1,0:T(1,128)}, u32[]{:S(2)}) copy-start(f32[1,256]{1,0:T(1,128)} %get-tuple-element.11) | copy-start | bytes 3076

commit v3 on v2

--- a/solution.py
+++ b/solution.py
@@ -407,12 +407,10 @@
     fa_column = column_of(fa_row)
     for j in range(0, fine, LANES):
         h1r[:, j : j + LANES] = lanes_hot(fa_column, j)
-    for h in range(chunks):
-        relay(h)
-
     fine_copies = []
     local_copies = []
     for h in range(chunks):
+        relay(h)
         arrive(relay_copies[h])
         columns = pl.ds(pl.multiple_of(me * share + h * LANES, LANES), LANES)
         means2 = base2[:, chunk_of(h)] + pull2[...] * dot(means3[h], h23[...]).T
@@ -495,6 +493,29 @@
         copy.wait_send()
 
 
+def land(count, *refs):
+    sem = refs[-1]
+    pairs = zip(refs[:count], refs[count : 2 * count])
+    copies = [pltpu.make_async_copy(a, b, sem.at[i]) for i, (a, b) in enumerate(pairs)]
+    for copy in copies:
+        copy.start()
+    for copy in copies:
+        copy.wait()
+
+
+def settle(*arrays):
+    count = len(arrays)
+    return pl.pallas_call(
+        functools.partial(land, count),
+        out_shape=tuple(jax.ShapeDtypeStruct(a.shape, a.dtype) for a in arrays),
+        in_specs=[pl.BlockSpec(memory_space=pltpu.VMEM)] * count,
+        out_specs=tuple([pl.BlockSpec(memory_space=pl.ANY)] * count),
+        scratch_shapes=[pltpu.SemaphoreType.DMA((count,))],
+        compiler_params=pltpu.CompilerParams(vmem_limit_bytes=4 << 20),
+        name="settle",
+    )(*arrays)
+
+
 def fused(rows, fine_assign, parent1, parent2, parent3, shrink):
     n = lax.axis_size("clus")
     m = lax.axis_size("dp")
@@ -520,7 +541,7 @@
             jax.ShapeDtypeStruct((1, fine_dev), F32),
         ),
         in_specs=[vmem] * 4
-        + [pl.BlockSpec(memory_space=pltpu.SMEM), pl.BlockSpec(memory_space=pl.ANY)],
+        + [pl.BlockSpec(memory_space=pltpu.SMEM), pl.BlockSpec(memory_space=pltpu.HBM)],
         out_specs=[vmem] * 4,
         scratch_shapes=[
             pltpu.VMEM((n, 1, count), jnp.int32),
@@ -570,7 +591,7 @@
             dma((3 + chunks,)),
         ],
         compiler_params=pltpu.CompilerParams(
-            collective_id=0, has_side_effects=True, vmem_limit_bytes=60 << 20
+            collective_id=0, has_side_effects=True, vmem_limit_bytes=32 << 20
         ),
         name="sweep",
     )(
@@ -581,6 +602,7 @@
         shrink,
         rows,
     )
+    fine_out, mid_out, coarse_out, spread = settle(fine_out, mid_out, coarse_out, spread)
     return fine_out, mid_out, coarse_out, spread.reshape(fine_dev)
 
 

time: 42.3 us -> 38.6 us (0.913)
  local copies, waits for them, and re-layouts: 3.89 us -> 1.73 us
  Pallas kernels: 37.5 us -> 36 us
    pallas_call x1, Pallas kernels: 37.5 us -> 35.1 us  [fused(): pl.pallas_call(functools.partial(sweep, n, m), out_shape=(jax.ShapeDtypeS...]
    unnamed x10 -> x12, local copies, waits for them, and re-layouts: 3.89 us -> 1.73 us
    pallas_call x0 -> x1, Pallas kernels: none -> 0.87 us  [settle(): pl.pallas_call(functools.partial(land, count), out_shape=tuple((jax.Shape...]
where the time goes in v3:
time: 38.6 us; the launch traced here: 38.4 us
  Pallas kernels  36 us (93%)
  local copies, waits for them, and re-layouts  1.73 us (4%)
  between operations  0.68 us (2%)
    pallas_call x1, Pallas kernels, fused(): pl.pallas_call(functools.partial(sweep, n, m), out_shape=(jax.ShapeDtypeS...  35.1 us
    unnamed x12, local copies, waits for them, and re-layouts  1.73 us
    pallas_call x1, Pallas kernels, settle(): pl.pallas_call(functools.partial(land, count), out_shape=tuple((jax.Shape...  0.87 us

profile of v3, /device:TPU:0, one launch (start us, length us, event | category | flops | bytes accessed | tf_op | source)
XLA Modules:
  0.0 38.4 jit_solution(11122092519371069998)
XLA Ops:
  0.6 0.0 copy-start.3
  0.6 0.0 copy-start.4
  0.7 0.0 copy-start.1
  0.7 0.0 copy-start.2
  0.7 0.0 copy-start.5
  0.7 0.6 %copy-done.3 = s32[256]{0:T(256)S(1)} copy-done((s32[256]{0:T(256)S(1)}, s32[256]{0:T(256)}, u32[]{:S(2)}) %copy-start.3) | copy-done | bytes 1048
  1.3 0.0 copy-done.4
  1.3 0.0 copy-done.1
  1.3 0.0 copy-done.2
  1.4 0.0 copy-done.5
  1.4 0.0 copy-start
  1.4 1.0 %copy-done = bf16[256,1024]{1,0:T(8,128)(2,1)S(1)} copy-done((bf16[256,1024]{1,0:T(8,128)(2,1)S(1)}, bf16[256,1024]{1,0:T(8,128)(2,1)}, u32[]{:S(2)}) %copy-start) | copy-done | bytes 524312
  2.4 35.1 %sweep.1 = (bf16[256,1024]{1,0:T(8,128)(2,1)S(1)}, bf16[64,1024]{1,0:T(8,128)(2,1)S(1)}, bf16[16,1024]{1,0:T(8,128)(2,1)S(1)}, f32[1,256]{1,0:T(1,128)S(1)}) custom-call(s32[1,256]{1,0:T(1,128)S(1)} %bitcast.6, s32[1,256]{1,0:T(1,128)S(1)} %bitcast.7, s32[1,256]{1,0:T(1,128)S(1)} %bitcast.8, s32[1,512]{1,0:T(1,128)S(1)} %bitcast.5, f32[4]{0:T(128)S(1)} %copy-done.5, ...), custom_call_target="tpu_custom_call" | custom-call | tf_op jit(solution)/shard_map/sweep/pallas_call | solution.py:535
  37.6 0.9 %settle.1 = (bf16[256,1024]{1,0:T(8,128)(2,1)}, bf16[64,1024]{1,0:T(8,128)(2,1)}, bf16[16,1024]{1,0:T(8,128)(2,1)}, f32[1,256]{1,0:T(1,128)}) custom-call(bf16[256,1024]{1,0:T(8,128)(2,1)S(1)} %get-tuple-element.12.refs_0_, bf16[64,1024]{1,0:T(8,128)(2,1)S(1)} %get-tuple-element.13.refs_1_, bf16[16,1024]{1,0:T(8,128)(2,1)S(1)} %get-tuple-element.14.refs_2_, ...), custom_call_target="tpu_custom_call" | custom-call | tf_op jit(solution)/shard_map/settle/pallas_call | solution.py:508
Async XLA Ops:
  0.6 0.7 %copy-start.3 = (s32[256]{0:T(256)S(1)}, s32[256]{0:T(256)}, u32[]{:S(2)}) copy-start(s32[256]{0:T(256)} %param.8) | copy-start | bytes 3076
  0.6 0.7 %copy-start.4 = (s32[256]{0:T(256)S(1)}, s32[256]{0:T(256)}, u32[]{:S(2)}) copy-start(s32[256]{0:T(256)} %param.9) | copy-start | bytes 3076
  0.7 0.7 %copy-start.1 = (s32[512]{0:T(512)S(1)}, s32[512]{0:T(512)}, u32[]{:S(2)}) copy-start(s32[512]{0:T(512)} %param.10) | copy-start | bytes 6148
  0.7 0.7 %copy-start.2 = (s32[256]{0:T(256)S(1)}, s32[256]{0:T(256)}, u32[]{:S(2)}) copy-start(s32[256]{0:T(256)} %param.7) | copy-start | bytes 3076
  0.7 0.7 %copy-start.5 = (f32[4]{0:T(128)S(1)}, f32[4]{0:T(128)}, u32[]{:S(2)}) copy-start(f32[4]{0:T(128)} %shrink_ref.1) | copy-start | bytes 52
  1.4 1.0 %copy-start = (bf16[256,1024]{1,0:T(8,128)(2,1)S(1)}, bf16[256,1024]{1,0:T(8,128)(2,1)}, u32[]{:S(2)}) copy-start(bf16[256,1024]{1,0:T(8,128)(2,1)} %rows_ref.1) | copy-start | bytes 1572868

commit v4 on v3

--- a/solution.py
+++ b/solution.py
@@ -600,7 +600,7 @@
         parent2.reshape(1, middle),
         parent3.reshape(1, third),
         shrink,
-        rows,
+        pltpu.with_memory_space_constraint(rows, pltpu.HBM),
     )
     fine_out, mid_out, coarse_out, spread = settle(fine_out, mid_out, coarse_out, spread)
     return fine_out, mid_out, coarse_out, spread.reshape(fine_dev)

time: 38.6 us -> 37.7 us (0.977)
  local copies, waits for them, and re-layouts: 1.73 us -> 0.69 us
    unnamed x12 -> x10, local copies, waits for them, and re-layouts: 1.73 us -> 0.69 us
where the time goes in v4:
time: 37.7 us; the launch traced here: 37.5 us
  Pallas kernels  36.2 us (96%)
  local copies, waits for them, and re-layouts  0.69 us (2%)
  between operations  0.68 us (2%)
    pallas_call x1, Pallas kernels, fused(): pl.pallas_call(functools.partial(sweep, n, m), out_shape=(jax.ShapeDtypeS...  35.3 us
    pallas_call x1, Pallas kernels, settle(): pl.pallas_call(functools.partial(land, count), out_shape=tuple((jax.Shape...  0.87 us

profile of v4, /device:TPU:0, one launch (start us, length us, event | category | flops | bytes accessed | tf_op | source)
XLA Modules:
  0.0 37.5 jit_solution(11077513373068928068)
XLA Ops:
  0.6 0.0 copy-start.2
  0.6 0.0 copy-start.3
  0.7 0.0 copy-start
  0.7 0.0 copy-start.1
  0.7 0.0 copy-start.4
  0.7 0.6 %copy-done.2 = s32[256]{0:T(256)S(1)} copy-done((s32[256]{0:T(256)S(1)}, s32[256]{0:T(256)}, u32[]{:S(2)}) %copy-start.2) | copy-done | bytes 1048
  1.3 0.0 copy-done.3
  1.3 0.0 copy-done
  1.3 0.0 copy-done.1
  1.4 0.0 copy-done.4
  1.4 35.3 %sweep.1 = (bf16[256,1024]{1,0:T(8,128)(2,1)S(1)}, bf16[64,1024]{1,0:T(8,128)(2,1)S(1)}, bf16[16,1024]{1,0:T(8,128)(2,1)S(1)}, f32[1,256]{1,0:T(1,128)S(1)}) custom-call(s32[1,256]{1,0:T(1,128)S(1)} %bitcast.6, s32[1,256]{1,0:T(1,128)S(1)} %bitcast.7, s32[1,256]{1,0:T(1,128)S(1)} %bitcast.8, s32[1,512]{1,0:T(1,128)S(1)} %bitcast.5, f32[4]{0:T(128)S(1)} %copy-done.4, ...), custom_call_target="tpu_custom_call" | custom-call | tf_op jit(solution)/shard_map/sweep/pallas_call | solution.py:535
  36.7 0.9 %settle.1 = (bf16[256,1024]{1,0:T(8,128)(2,1)}, bf16[64,1024]{1,0:T(8,128)(2,1)}, bf16[16,1024]{1,0:T(8,128)(2,1)}, f32[1,256]{1,0:T(1,128)}) custom-call(bf16[256,1024]{1,0:T(8,128)(2,1)S(1)} %get-tuple-element.12.refs_0_, bf16[64,1024]{1,0:T(8,128)(2,1)S(1)} %get-tuple-element.13.refs_1_, bf16[16,1024]{1,0:T(8,128)(2,1)S(1)} %get-tuple-element.14.refs_2_, ...), custom_call_target="tpu_custom_call" | custom-call | tf_op jit(solution)/shard_map/settle/pallas_call | solution.py:508
Async XLA Ops:
  0.6 0.7 %copy-start.2 = (s32[256]{0:T(256)S(1)}, s32[256]{0:T(256)}, u32[]{:S(2)}) copy-start(s32[256]{0:T(256)} %param.8) | copy-start | bytes 3076
  0.6 0.7 %copy-start.3 = (s32[256]{0:T(256)S(1)}, s32[256]{0:T(256)}, u32[]{:S(2)}) copy-start(s32[256]{0:T(256)} %param.9) | copy-start | bytes 3076
  0.7 0.7 %copy-start = (s32[512]{0:T(512)S(1)}, s32[512]{0:T(512)}, u32[]{:S(2)}) copy-start(s32[512]{0:T(512)} %param.10) | copy-start | bytes 6148
  0.7 0.7 %copy-start.1 = (s32[256]{0:T(256)S(1)}, s32[256]{0:T(256)}, u32[]{:S(2)}) copy-start(s32[256]{0:T(256)} %param.7) | copy-start | bytes 3076
  0.7 0.7 %copy-start.4 = (f32[4]{0:T(128)S(1)}, f32[4]{0:T(128)}, u32[]{:S(2)}) copy-start(f32[4]{0:T(128)} %shrink_ref.1) | copy-start | bytes 52
